TPU v7x, 256 devices: a whole 4x4x8 slice. The times are simulated.
256 devices in a mesh: pipe: 8 (over z_lo, y), dp: 32 (over x, z_hi, core).
Axes of the slice: x: 4, y: 4, z: 8 (z_hi: 4, z_lo: 2; z = z_hi * 2 + z_lo), core: 2. Of those that a mesh axis runs over, the one named last changes fastest.
Arguments:
- inputs: bfloat16 [2, 4096, 2048], P(None, 'dp'), may hold values from -6 to 6
- cotangent: bfloat16 [2, 4096, 2048], P(None, 'dp'), may hold values from -0.125 to 0.125
- joined: int32 [2, 16], replicated, may hold values 0 or 1
- w_qkv: bfloat16 [8, 2048, 1536], P('pipe', 'dp'), may hold values from -0.125 to 0.125
- w_out: bfloat16 [8, 1024, 2048], P('pipe', 'dp'), may hold values from -0.1875 to 0.1875
Outputs:
- grad_qkv: float32 [8, 2048, 1536], P('pipe', 'dp')
- grad_out: float32 [8, 1024, 2048], P('pipe', 'dp')
Inputs may be any that keep to these rules, and one draw needn't show every extreme that they name: joined[m, j] is 1 where bin j of micro-batch m holds one molecule covering both of its blocks, 0 where each block holds its own molecule.
All inputs are finite; a program needn't handle non-finite values.
Results may differ from a plain program's by a relative error of at most 0.028.
Values may be sent and summed in bfloat16 or wider, within the bound.
No kernel may reach another device: no remote copies, remote signals or barrier semaphores. Data moves between devices by JAX's collectives and lax.ppermute only.
A program may use at most 192 MiB of HBM per device.

v0:
```python
import math
import jax
import jax.numpy as jnp
from jax import lax
from jax.sharding import PartitionSpec as P

HEADS = 16
HEAD = 64
KVH = 4
norm_eps = 1e-05


def from_partner(block, axis, apart):
    count = lax.axis_size(axis)
    route = []
    for low in range(count):
        high = low | 1 << apart
        if high != low and high < count:
            route += [(low, high), (high, low)]
    return lax.ppermute(block, axis, route)


def from_behind(value, axis, steps):
    count = lax.axis_size(axis)
    leading, last = (max(0, -steps), min(count, count - steps))
    return lax.ppermute(value, axis, [(source, source + steps) for source in range(leading, last)])


def normalize(hidden):
    widened = hidden.astype(jnp.float32)
    inv_rms = lax.rsqrt(jnp.mean(widened * widened, axis=-1, keepdims=True) + norm_eps)
    return (widened * inv_rms).astype(jnp.bfloat16)


def project(hidden, w_qkv):
    normed = normalize(hidden)
    projected = jnp.dot(normed, w_qkv, preferred_element_type=jnp.float32)
    inner_width = HEADS * HEAD
    kv_width = KVH * HEAD
    queries = projected[:, :inner_width].astype(jnp.bfloat16)
    own_kv = jnp.stack(
        [projected[:, inner_width : inner_width + kv_width], projected[:, inner_width + kv_width :]]
    ).astype(jnp.bfloat16)
    return (normed, queries, own_kv)


def attend(queries, key_rows, value_rows, visible):
    row_count = queries.shape[0]
    key_count = key_rows.shape[0]
    grouped = queries.astype(jnp.float32).reshape(row_count, KVH, HEADS // KVH, HEAD)
    key_heads = key_rows.astype(jnp.float32).reshape(key_count, KVH, HEAD)
    value_heads = value_rows.astype(jnp.float32).reshape(key_count, KVH, HEAD)
    scores = jnp.einsum("tkgd,ukd->kgtu", grouped, key_heads) * (1.0 / math.sqrt(HEAD))
    raised = jnp.exp(scores) * visible
    prob_rows = (raised / jnp.sum(raised, axis=-1, keepdims=True)).astype(jnp.bfloat16)
    prob_rows = lax.optimization_barrier(prob_rows)
    context = jnp.einsum("kgtu,ukd->tkgd", prob_rows.astype(jnp.float32), value_heads)
    return context.reshape(row_count, HEADS * HEAD).astype(jnp.bfloat16)


def attend_pair(queries, own_kv, pair_kv, joined_flag):
    row_count = own_kv.shape[1]
    pair_mask = jnp.where(joined_flag > 0, 1.0, 0.0).astype(jnp.float32) * jnp.ones(
        (row_count,), jnp.float32
    )
    visible = jnp.concatenate([jnp.ones((row_count,), jnp.float32), pair_mask])
    key_rows = jnp.concatenate([own_kv[0], pair_kv[0]])
    value_rows = jnp.concatenate([own_kv[1], pair_kv[1]])
    return attend(queries, key_rows, value_rows, visible)


def attention_choice(queries, own_kv, pair_kv, joined_flag):
    return attend_pair(queries, own_kv, pair_kv, joined_flag)


def finish(hidden, context, w_out):
    return (
        hidden.astype(jnp.float32) + jnp.dot(context, w_out, preferred_element_type=jnp.float32)
    ).astype(jnp.bfloat16)


def attention_grads(upstream, queries, own_kv, pair_kv, joined_flag, w_out):
    d_context = jnp.dot(upstream, w_out.T, preferred_element_type=jnp.float32).astype(jnp.bfloat16)

    def forward_part(query_rows, own_rows, pair_rows):
        return attention_choice(query_rows, own_rows, pair_rows, joined_flag)

    unused, pull = jax.vjp(forward_part, queries, own_kv, pair_kv)
    return pull(d_context)


def input_grads(upstream, hidden, d_query, d_own, back_kv, w_qkv):
    combined = (d_own.astype(jnp.float32) + back_kv.astype(jnp.float32)).astype(jnp.bfloat16)
    d_proj = jnp.concatenate([d_query, combined[0], combined[1]], axis=-1)
    d_normed = jnp.dot(d_proj, w_qkv.T, preferred_element_type=jnp.float32)
    widened = hidden.astype(jnp.float32)
    inv_rms = lax.rsqrt(jnp.mean(widened * widened, axis=-1, keepdims=True) + norm_eps)
    cubed = inv_rms * inv_rms * inv_rms
    d_widened = inv_rms * d_normed - widened * cubed * jnp.mean(
        d_normed * widened, axis=-1, keepdims=True
    )
    previous = (upstream.astype(jnp.float32) + d_widened).astype(jnp.bfloat16)
    return (d_proj, previous)


def keep_slot(store, value, slot_index, active):
    current = lax.dynamic_index_in_dim(store, slot_index, 0, keepdims=False)
    return lax.dynamic_update_index_in_dim(store, jnp.where(active, value, current), slot_index, 0)


def on_device(inputs, cotangent, joined, w_qkv, w_out):
    segments = lax.axis_size("pipe")
    segment_index = lax.axis_index("pipe")
    member = lax.axis_index("dp")
    micro_count = inputs.shape[0]
    row_count = inputs.shape[1]
    model_width = inputs.shape[2]
    full_qkv, full_out = (
        lax.all_gather(w_qkv[0], "dp", axis=0, tiled=True),
        lax.all_gather(w_out[0], "dp", axis=0, tiled=True),
    )
    inner_width = full_out.shape[0]
    proj_width = full_qkv.shape[1]
    kv_width = (proj_width - inner_width) // 2
    bin_flags = lax.dynamic_index_in_dim(joined, member // 2, 1, keepdims=False)
    turn_count = micro_count + segments - 1
    blank_rows = jnp.zeros((row_count, model_width), jnp.bfloat16)
    blank_query = jnp.zeros((row_count, inner_width), jnp.bfloat16)
    blank_kv = jnp.zeros((2, row_count, kv_width), jnp.bfloat16)
    blank_proj = jnp.zeros((row_count, proj_width), jnp.bfloat16)
    stores = tuple(
        (
            jnp.zeros((micro_count,) + shaped.shape, jnp.bfloat16)
            for shaped in (blank_rows, blank_rows, blank_query, blank_kv, blank_kv, blank_query)
        )
    )

    def forward_step(turn, incoming, saved):
        position = turn - segment_index
        active = (position >= 0) & (position < micro_count)
        slot_index = jnp.clip(position, 0, micro_count - 1)
        fresh_rows = lax.dynamic_index_in_dim(
            inputs, jnp.clip(turn, 0, micro_count - 1), 0, keepdims=False
        )
        hidden = jnp.where(segment_index == 0, fresh_rows, incoming)
        joined_flag = bin_flags[slot_index]

        def run_project(state):
            return project(state, full_qkv)

        def skip_project(state):
            return (blank_rows, blank_query, blank_kv)

        normed, queries, own_kv = lax.cond(active, run_project, skip_project, hidden)
        pair_kv = from_partner(own_kv, "dp", 0)

        def run_attend(operands):
            context = attention_choice(operands[0], operands[1], operands[2], joined_flag)
            return (context, finish(operands[3], context, full_out))

        def skip_attend(operands):
            return (blank_query, blank_rows)

        context, result = lax.cond(
            active, run_attend, skip_attend, (queries, own_kv, pair_kv, hidden)
        )
        fresh_values = (hidden, normed, queries, own_kv, pair_kv, context)
        saved = tuple(
            (
                keep_slot(store, value, slot_index, active)
                for store, value in zip(saved, fresh_values)
            )
        )
        return (result, saved)

    def forward_turn(turn, carry):
        result, new_stores = forward_step(turn, carry[0], carry[1])
        return (from_behind(result, "pipe", 1), new_stores)

    carry = lax.fori_loop(0, turn_count - 1, forward_turn, (blank_rows, stores))
    unused, stores = forward_step(turn_count - 1, carry[0], carry[1])
    ledger = (jnp.zeros(full_qkv.shape, jnp.float32), jnp.zeros(full_out.shape, jnp.float32))

    def backward_step(turn, incoming, tally):
        position = turn - (segments - 1 - segment_index)
        active = (position >= 0) & (position < micro_count)
        slot_index = jnp.clip(position, 0, micro_count - 1)
        fresh_rows = lax.dynamic_index_in_dim(
            cotangent, jnp.clip(turn, 0, micro_count - 1), 0, keepdims=False
        )
        upstream = jnp.where(segment_index == segments - 1, fresh_rows, incoming)
        hidden, normed, queries, own_kv, pair_kv, context = tuple(
            (lax.dynamic_index_in_dim(store, slot_index, 0, keepdims=False) for store in stores)
        )
        joined_flag = bin_flags[slot_index]

        def run_first(state):
            return attention_grads(state, queries, own_kv, pair_kv, joined_flag, full_out)

        def skip_first(state):
            return (blank_query, blank_kv, blank_kv)

        d_query, d_own, d_pair = lax.cond(active, run_first, skip_first, upstream)
        back_kv = from_partner(d_pair, "dp", 0)

        def run_second(operands):
            return input_grads(operands[0], hidden, operands[1], operands[2], operands[3], full_qkv)

        def skip_second(operands):
            return (blank_proj, blank_rows)

        d_proj, previous = lax.cond(
            active, run_second, skip_second, (upstream, d_query, d_own, back_kv)
        )

        def run_terms(totals):
            qkv_total = totals[0] + jnp.dot(normed.T, d_proj, preferred_element_type=jnp.float32)
            out_total = totals[1] + jnp.dot(context.T, upstream, preferred_element_type=jnp.float32)
            return (qkv_total, out_total)

        def skip_terms(totals):
            return totals

        tally = lax.cond(active, run_terms, skip_terms, tally)
        return (previous, tally)

    def backward_turn(turn, carry):
        previous, new_tally = backward_step(turn, carry[0], carry[1])
        return (from_behind(previous, "pipe", -1), new_tally)

    carry = lax.fori_loop(0, turn_count - 1, backward_turn, (blank_rows, ledger))
    unused, ledger = backward_step(turn_count - 1, carry[0], carry[1])
    grad_qkv, grad_out = (
        lax.psum_scatter(
            ledger[0].astype(jnp.bfloat16), "dp", scatter_dimension=0, tiled=True
        ).astype(jnp.float32),
        lax.psum_scatter(
            ledger[1].astype(jnp.bfloat16), "dp", scatter_dimension=0, tiled=True
        ).astype(jnp.float32),
    )
    return (grad_qkv[None], grad_out[None])


def solution(mesh):
    return jax.shard_map(
        on_device,
        mesh=mesh,
        in_specs=(
            P(None, "dp", None),
            P(None, "dp", None),
            P(),
            P("pipe", "dp", None),
            P("pipe", "dp", None),
        ),
        out_specs=(P("pipe", "dp", None), P("pipe", "dp", None)),
        check_vma=False,
    )
```

profile of v0, /device:TPU:1, one launch (start us, length us, event | category | flops | bytes accessed | tf_op | source)
XLA Modules:
  0.0 1105.0 jit_solution(1348793310206374245)
XLA Ops:
  10.2 65.1 %all-gather.5.cloned.1.call-done = bf16[1,1024,2048]{2,1,0:T(8,128)(2,1)} async-done(((bf16[1,32,2048]{2,1,0:T(8,128)(2,1)}), bf16[1,1024,2048]{2,1,0:T(8,128)(2,1)}) %all-gather.5.cloned.1.call-update) | async-done | bytes 4194320 | tf_op jit(solution)/shard_map/all_gather | solution.py:120
  75.2 69.0 %all-gather.7.cloned.1.call-done = bf16[1,2048,1536]{2,1,0:T(8,128)(2,1)} async-done(((bf16[1,64,1536]{2,1,0:T(8,128)(2,1)}), bf16[1,2048,1536]{2,1,0:T(8,128)(2,1)}) %all-gather.7.cloned.1.call-update) | async-done | bytes 6291472 | tf_op jit(solution)/shard_map/all_gather | solution.py:119
  148.2 266.3 %while.45 = (s32[]{:T(128)}, bf16[128,2048]{1,0:T(8,128)(2,1)S(1)}, bf16[2,128,2048]{2,1,0:T(8,128)(2,1)}, bf16[2,128,2048]{2,1,0:T(8,128)(2,1)}, bf16[2,128,102...) while((s32[]{:T(128)}, bf16[128,2048]{1,0:T(8,128)(2,1)S(1)}, ...), condition=%wide.region_7.8_spmd, body=%wide.region_0.7_spmd.sunk | while | flops 1484519552 | bytes 54158364 | solution.py:180
  151.4 6.9 conditional.20
  152.6 4.0 convolution_convert_fusion
  163.7 7.8 conditional.21
  175.5 8.6 collective-permute-done.1
  187.4 6.9 conditional.20
  188.5 4.0 convolution_convert_fusion
  200.1 7.8 conditional.21
  207.9 4.1 collective-permute-start.1
  214.8 8.6 collective-permute-done.1
  233.8 17.5 %collective-permute-start.1 = (bf16[128,2048]{1,0:T(8,128)(2,1)S(1)}, bf16[128,2048]{1,0:T(8,128)(2,1)S(1)}, u32[]{:S(2)}, u32[]{:S(2)}) collective-permute-start(bf16[128,2048]{1,0:T(8,128)(2,1)S(1)} %get-tuple-element.1417), channel_id=1, source_target_pairs={{0,32},{32,64},{64,96},{96,128},{128,160},{160,192},{192,224},{1,3... | collective-permute-start | bytes 1572872 | tf_op jit(solution)/shard_map/while/body/eval_jaxpr/ppermute | solution.py:26
  253.1 9.5 collective-permute-done.1
  273.1 4.1 collective-permute-start.1
  279.0 9.5 collective-permute-done.1
  299.0 15.3 %collective-permute-start.1 = (bf16[128,2048]{1,0:T(8,128)(2,1)S(1)}, bf16[128,2048]{1,0:T(8,128)(2,1)S(1)}, u32[]{:S(2)}, u32[]{:S(2)}) collective-permute-start(bf16[128,2048]{1,0:T(8,128)(2,1)S(1)} %get-tuple-element.1417), channel_id=1, source_target_pairs={{0,32},{32,64},{64,96},{96,128},{128,160},{160,192},{192,224},{1,3... | collective-permute-start | bytes 1572872 | tf_op jit(solution)/shard_map/while/body/eval_jaxpr/ppermute | solution.py:26
  316.1 9.5 collective-permute-done.1
  336.1 4.1 collective-permute-start.1
  342.0 9.5 collective-permute-done.1
  362.0 15.3 %collective-permute-start.1 = (bf16[128,2048]{1,0:T(8,128)(2,1)S(1)}, bf16[128,2048]{1,0:T(8,128)(2,1)S(1)}, u32[]{:S(2)}, u32[]{:S(2)}) collective-permute-start(bf16[128,2048]{1,0:T(8,128)(2,1)S(1)} %get-tuple-element.1417), channel_id=1, source_target_pairs={{0,32},{32,64},{64,96},{96,128},{128,160},{160,192},{192,224},{1,3... | collective-permute-start | bytes 1572872 | tf_op jit(solution)/shard_map/while/body/eval_jaxpr/ppermute | solution.py:26
  379.1 9.5 collective-permute-done.1
  399.1 4.1 collective-permute-start.1
  405.0 9.5 collective-permute-done.1
  428.2 6.2 broadcast_in_dim.196
  434.4 4.3 broadcast_in_dim.197
  439.5 403.7 %while.46 = (s32[]{:T(128)}, bf16[128,2048]{1,0:T(8,128)(2,1)}, f32[2048,1536]{1,0:T(8,128)}, f32[1024,2048]{1,0:T(8,128)}, s32[]{:T(128)}, /*index=5*/pred[]{:T...) while((s32[]{:T(128)}, bf16[128,2048]{1,0:T(8,128)(2,1)}, ...), condition=%wide.region_25.26_spmd, body=%wide.region_14.25_spmd.sunk | while | flops 3045198336 | bytes 92394472 | solution.py:231
  446.2 30.4 %collective-permute-done.3 = bf16[128,2048]{1,0:T(8,128)(2,1)} collective-permute-done((bf16[128,2048]{1,0:T(8,128)(2,1)S(1)}, bf16[128,2048]{1,0:T(8,128)(2,1)}, u32[]{:S(2)}, u32[]{:S(2)}) %collective-permute-start.3) | collective-permute-done | bytes 524320 | tf_op jit(solution)/shard_map/while/body/eval_jaxpr/ppermute | solution.py:26
  483.7 17.0 %collective-permute-done.3 = bf16[128,2048]{1,0:T(8,128)(2,1)} collective-permute-done((bf16[128,2048]{1,0:T(8,128)(2,1)S(1)}, bf16[128,2048]{1,0:T(8,128)(2,1)}, u32[]{:S(2)}, u32[]{:S(2)}) %collective-permute-start.3) | collective-permute-done | bytes 524320 | tf_op jit(solution)/shard_map/while/body/eval_jaxpr/ppermute | solution.py:26
  507.9 23.9 %collective-permute-done.3 = bf16[128,2048]{1,0:T(8,128)(2,1)} collective-permute-done((bf16[128,2048]{1,0:T(8,128)(2,1)S(1)}, bf16[128,2048]{1,0:T(8,128)(2,1)}, u32[]{:S(2)}, u32[]{:S(2)}) %collective-permute-start.3) | collective-permute-done | bytes 524320 | tf_op jit(solution)/shard_map/while/body/eval_jaxpr/ppermute | solution.py:26
  539.0 17.0 %collective-permute-done.3 = bf16[128,2048]{1,0:T(8,128)(2,1)} collective-permute-done((bf16[128,2048]{1,0:T(8,128)(2,1)S(1)}, bf16[128,2048]{1,0:T(8,128)(2,1)}, u32[]{:S(2)}, u32[]{:S(2)}) %collective-permute-start.3) | collective-permute-done | bytes 524320 | tf_op jit(solution)/shard_map/while/body/eval_jaxpr/ppermute | solution.py:26
  563.2 23.9 %collective-permute-done.3 = bf16[128,2048]{1,0:T(8,128)(2,1)} collective-permute-done((bf16[128,2048]{1,0:T(8,128)(2,1)S(1)}, bf16[128,2048]{1,0:T(8,128)(2,1)}, u32[]{:S(2)}, u32[]{:S(2)}) %collective-permute-start.3) | collective-permute-done | bytes 524320 | tf_op jit(solution)/shard_map/while/body/eval_jaxpr/ppermute | solution.py:26
  594.3 16.2 %collective-permute-done.3 = bf16[128,2048]{1,0:T(8,128)(2,1)} collective-permute-done((bf16[128,2048]{1,0:T(8,128)(2,1)S(1)}, bf16[128,2048]{1,0:T(8,128)(2,1)}, u32[]{:S(2)}, u32[]{:S(2)}) %collective-permute-start.3) | collective-permute-done | bytes 524320 | tf_op jit(solution)/shard_map/while/body/eval_jaxpr/ppermute | solution.py:26
  617.8 176.7 %collective-permute-done.3 = bf16[128,2048]{1,0:T(8,128)(2,1)} collective-permute-done((bf16[128,2048]{1,0:T(8,128)(2,1)S(1)}, bf16[128,2048]{1,0:T(8,128)(2,1)}, u32[]{:S(2)}, u32[]{:S(2)}) %collective-permute-start.3) | collective-permute-done | bytes 524320 | tf_op jit(solution)/shard_map/while/body/eval_jaxpr/ppermute | solution.py:26
  795.8 15.6 %conditional.22 = (bf16[128,1024]{0,1:T(8,128)(2,1)}, bf16[2,128,256]{1,2,0:T(8,128)(2,1)S(1)}, bf16[2,128,256]{1,2,0:T(8,128)(2,1)}) conditional(s32[]{:T(128)} %convert_element_type.320, () %tuple.239, (bf16[128,2048]{1,0:T(8,128)(2,1)S(1)}, bf16[1024,2048]{1,0:T(8,128)(2,1)}, bf16[2,2,128,256]{2,3,1,0:T(8,128)(2,1)S(1)}, s32[]{:T(128)}, ...), branch_computations={%region_15.15_spmd, %region_16.18_spmd} | conditional | flops 887359488 | bytes 25934138 | solution.py:203
  814.4 8.2 conditional.23
  815.7 5.2 fusion.41
  823.9 19.2 %conditional.24 = ((f32[2048,1536]{1,0:T(8,128)}, f32[1024,2048]{1,0:T(8,128)})) conditional(s32[]{:T(128)} %convert_element_type.320, (f32[2048,1536]{1,0:T(8,128)}, f32[1024,2048]{1,0:T(8,128)}) %tuple.242, (bf16[2,128,2048]{2,1,0:T(8,128)(2,1)}, s32[]{:T(128)}, bf16[128,1536]{1,0:T(8,128)(2,1)S(1)}, f32[2048,1536]{1,0:T(8,128)}, ...), branch_computations={%region_23.23_spmd, %region_24.24_spmd} | conditional | flops 1347420160 | bytes 43648024 | solution.py:224
  823.9 11.2 %convolution_add_fusion.1 = f32[2048,1536]{1,0:T(8,128)} fusion(f32[2048,1536]{1,0:T(8,128)} %get-tuple-element.966, bf16[128,1536]{1,0:T(8,128)(2,1)S(1)} %get-tuple-element.969, bf16[2,128,2048]{2,1,0:T(8,128)(2,1)} %get-tuple-element.967, s32[]{:T(128)} %get-tuple-element.968), kind=kOutput, calls=%fused_computation.121 | convolution fusion | flops 808452096 | bytes 26083840 | tf_op jit(solution)/shard_map/while/body/eval_jaxpr/cond/branch_1_fun/dot_general | solution.py:217
  835.1 8.0 convolution_add_fusion.2
  844.5 16.6 %conditional.12 = (bf16[128,1024]{0,1:T(8,128)(2,1)}, bf16[2,128,256]{1,2,0:T(8,128)(2,1)}, bf16[2,128,256]{1,2,0:T(8,128)(2,1)}) conditional(s32[]{:T(128)} %convert_element_type.228, () %tuple.147, (bf16[128,2048]{1,0:T(8,128)(2,1)S(1)}, bf16[1024,2048]{1,0:T(8,128)(2,1)}, bf16[2,2,128,256]{2,3,1,0:T(8,128)(2,1)S(1)}, s32[]{:T(128)}, ...), branch_computations={%region_26.27_spmd, %region_27.30_spmd} | conditional | flops 887359488 | bytes 25934154 | solution.py:203
  866.2 19.2 %conditional.14 = ((f32[2048,1536]{1,0:T(8,128)}, f32[1024,2048]{1,0:T(8,128)})) conditional(s32[]{:T(128)} %convert_element_type.228, (f32[2048,1536]{1,0:T(8,128)}, f32[1024,2048]{1,0:T(8,128)}) %tuple.145, (bf16[2,128,2048]{2,1,0:T(8,128)(2,1)}, s32[]{:T(128)}, bf16[128,1536]{1,0:T(8,128)(2,1)S(1)}, f32[2048,1536]{1,0:T(8,128)}, ...), branch_computations={%region_32.33_spmd, %region_33.34_spmd} | conditional | flops 1347420160 | bytes 43648024 | solution.py:224
  866.2 11.2 %convolution_add_fusion.3 = f32[2048,1536]{1,0:T(8,128)} fusion(f32[2048,1536]{1,0:T(8,128)} %get-tuple-element.1008, bf16[128,1536]{1,0:T(8,128)(2,1)S(1)} %get-tuple-element.1011, bf16[2,128,2048]{2,1,0:T(8,128)(2,1)} %get-tuple-element.1009, s32[]{:T(128)} %get-tuple-element.1010), kind=kOutput, calls=%fused_computation.172 | convolution fusion | flops 808452096 | bytes 26083840 | tf_op jit(solution)/shard_map/cond/branch_1_fun/dot_general | solution.py:217
  877.4 8.0 convolution_add_fusion.4
  885.4 6.1 convert_element_type.231
  891.5 8.0 convert_element_type.230
  899.5 85.3 %reduce-scatter.5.cloned.1.call-done = bf16[32,2048]{1,0:T(8,128)(2,1)} async-done(((bf16[1024,2048]{1,0:T(8,128)(2,1)}), bf16[32,2048]{1,0:T(8,128)(2,1)}) %reduce-scatter.5.cloned.1.call-update) | async-done | bytes 131088 | tf_op jit(solution)/shard_map/reduce_scatter | solution.py:237
  986.4 110.4 %reduce-scatter.3.cloned.1.call-done = bf16[64,1536]{1,0:T(8,128)(2,1)} async-done(((bf16[2048,1536]{1,0:T(8,128)(2,1)}), bf16[64,1536]{1,0:T(8,128)(2,1)}) %reduce-scatter.3.cloned.1.call-update) | async-done | bytes 196624 | tf_op jit(solution)/shard_map/reduce_scatter | solution.py:234
  (458 shorter events, 265.3 us)
Async XLA Ops:
  7.2 68.1 %all-gather.5.cloned.1.call-start = ((), (), s32[]{:S(2)}) async-start(), calls=%async_computation.4 | async-start | bytes 4325376 | tf_op jit(solution)/shard_map/all_gather | solution.py:120
  7.9 136.3 %all-gather.7.cloned.1.call-start = ((), (), s32[]{:S(2)}) async-start(), calls=%async_computation.5 | async-start | bytes 6488064 | tf_op jit(solution)/shard_map/all_gather | solution.py:119
  8.6 976.1 %reduce-scatter.5.cloned.1.call-start = ((), (), s32[]{:S(2)}) async-start(), calls=%async_computation.3 | async-start | bytes 4325376 | tf_op jit(solution)/shard_map/reduce_scatter | solution.py:237
  158.3 5.3 collective-permute-start
  171.5 12.7 %collective-permute-start.1 = (bf16[128,2048]{1,0:T(8,128)(2,1)S(1)}, bf16[128,2048]{1,0:T(8,128)(2,1)S(1)}, u32[]{:S(2)}, u32[]{:S(2)}) collective-permute-start(bf16[128,2048]{1,0:T(8,128)(2,1)S(1)} %get-tuple-element.1417), channel_id=1, source_target_pairs={{0,32},{32,64},{64,96},{96,128},{128,160},{160,192},{192,224},{1,3... | collective-permute-start | bytes 1572872 | tf_op jit(solution)/shard_map/while/body/eval_jaxpr/ppermute | solution.py:26
  194.3 5.9 collective-permute-start
  207.9 15.4 %collective-permute-start.1 = (bf16[128,2048]{1,0:T(8,128)(2,1)S(1)}, bf16[128,2048]{1,0:T(8,128)(2,1)S(1)}, u32[]{:S(2)}, u32[]{:S(2)}) collective-permute-start(bf16[128,2048]{1,0:T(8,128)(2,1)S(1)} %get-tuple-element.1417), channel_id=1, source_target_pairs={{0,32},{32,64},{64,96},{96,128},{128,160},{160,192},{192,224},{1,3... | collective-permute-start | bytes 1572872 | tf_op jit(solution)/shard_map/while/body/eval_jaxpr/ppermute | solution.py:26
  228.2 4.9 collective-permute-start
  233.8 28.8 %collective-permute-start.1 = (bf16[128,2048]{1,0:T(8,128)(2,1)S(1)}, bf16[128,2048]{1,0:T(8,128)(2,1)S(1)}, u32[]{:S(2)}, u32[]{:S(2)}) collective-permute-start(bf16[128,2048]{1,0:T(8,128)(2,1)S(1)} %get-tuple-element.1417), channel_id=1, source_target_pairs={{0,32},{32,64},{64,96},{96,128},{128,160},{160,192},{192,224},{1,3... | collective-permute-start | bytes 1572872 | tf_op jit(solution)/shard_map/while/body/eval_jaxpr/ppermute | solution.py:26
  267.4 4.9 collective-permute-start
  273.1 15.4 %collective-permute-start.1 = (bf16[128,2048]{1,0:T(8,128)(2,1)S(1)}, bf16[128,2048]{1,0:T(8,128)(2,1)S(1)}, u32[]{:S(2)}, u32[]{:S(2)}) collective-permute-start(bf16[128,2048]{1,0:T(8,128)(2,1)S(1)} %get-tuple-element.1417), channel_id=1, source_target_pairs={{0,32},{32,64},{64,96},{96,128},{128,160},{160,192},{192,224},{1,3... | collective-permute-start | bytes 1572872 | tf_op jit(solution)/shard_map/while/body/eval_jaxpr/ppermute | solution.py:26
  293.4 4.8 collective-permute-start
  299.0 26.6 %collective-permute-start.1 = (bf16[128,2048]{1,0:T(8,128)(2,1)S(1)}, bf16[128,2048]{1,0:T(8,128)(2,1)S(1)}, u32[]{:S(2)}, u32[]{:S(2)}) collective-permute-start(bf16[128,2048]{1,0:T(8,128)(2,1)S(1)} %get-tuple-element.1417), channel_id=1, source_target_pairs={{0,32},{32,64},{64,96},{96,128},{128,160},{160,192},{192,224},{1,3... | collective-permute-start | bytes 1572872 | tf_op jit(solution)/shard_map/while/body/eval_jaxpr/ppermute | solution.py:26
  330.4 4.8 collective-permute-start
  336.1 15.4 %collective-permute-start.1 = (bf16[128,2048]{1,0:T(8,128)(2,1)S(1)}, bf16[128,2048]{1,0:T(8,128)(2,1)S(1)}, u32[]{:S(2)}, u32[]{:S(2)}) collective-permute-start(bf16[128,2048]{1,0:T(8,128)(2,1)S(1)} %get-tuple-element.1417), channel_id=1, source_target_pairs={{0,32},{32,64},{64,96},{96,128},{128,160},{160,192},{192,224},{1,3... | collective-permute-start | bytes 1572872 | tf_op jit(solution)/shard_map/while/body/eval_jaxpr/ppermute | solution.py:26
  356.3 4.8 collective-permute-start
  362.0 26.6 %collective-permute-start.1 = (bf16[128,2048]{1,0:T(8,128)(2,1)S(1)}, bf16[128,2048]{1,0:T(8,128)(2,1)S(1)}, u32[]{:S(2)}, u32[]{:S(2)}) collective-permute-start(bf16[128,2048]{1,0:T(8,128)(2,1)S(1)} %get-tuple-element.1417), channel_id=1, source_target_pairs={{0,32},{32,64},{64,96},{96,128},{128,160},{160,192},{192,224},{1,3... | collective-permute-start | bytes 1572872 | tf_op jit(solution)/shard_map/while/body/eval_jaxpr/ppermute | solution.py:26
  393.4 4.8 collective-permute-start
  399.1 15.4 %collective-permute-start.1 = (bf16[128,2048]{1,0:T(8,128)(2,1)S(1)}, bf16[128,2048]{1,0:T(8,128)(2,1)S(1)}, u32[]{:S(2)}, u32[]{:S(2)}) collective-permute-start(bf16[128,2048]{1,0:T(8,128)(2,1)S(1)} %get-tuple-element.1417), channel_id=1, source_target_pairs={{0,32},{32,64},{64,96},{96,128},{128,160},{160,192},{192,224},{1,3... | collective-permute-start | bytes 1572872 | tf_op jit(solution)/shard_map/while/body/eval_jaxpr/ppermute | solution.py:26
  419.3 7.1 collective-permute-start.4
  443.3 1.4 collective-permute-start.2
  444.8 31.7 %collective-permute-start.3 = (bf16[128,2048]{1,0:T(8,128)(2,1)S(1)}, bf16[128,2048]{1,0:T(8,128)(2,1)}, u32[]{:S(2)}, u32[]{:S(2)}) collective-permute-start(bf16[128,2048]{1,0:T(8,128)(2,1)S(1)} %get-tuple-element.1444), channel_id=1, source_target_pairs={{32,0},{64,32},{96,64},{128,96},{160,128},{192,160},{224,192},{33,... | collective-permute-start | bytes 1572872 | tf_op jit(solution)/shard_map/while/body/eval_jaxpr/ppermute | solution.py:26
  446.1 30.4 %copy-start.4 = (bf16[2,2,128,256]{2,3,1,0:T(8,128)(2,1)S(1)}, bf16[2,2,128,256]{2,3,1,0:T(8,128)(2,1)}, u32[]{:S(2)}) copy-start(bf16[2,2,128,256]{2,3,1,0:T(8,128)(2,1)} %copy-done.3) | copy-start | bytes 786436 | tf_op jit(solution)/shard_map/while
  480.4 1.8 collective-permute-start.2
  482.3 18.3 %collective-permute-start.3 = (bf16[128,2048]{1,0:T(8,128)(2,1)S(1)}, bf16[128,2048]{1,0:T(8,128)(2,1)}, u32[]{:S(2)}, u32[]{:S(2)}) collective-permute-start(bf16[128,2048]{1,0:T(8,128)(2,1)S(1)} %get-tuple-element.1444), channel_id=1, source_target_pairs={{32,0},{64,32},{96,64},{128,96},{160,128},{192,160},{224,192},{33,... | collective-permute-start | bytes 1572872 | tf_op jit(solution)/shard_map/while/body/eval_jaxpr/ppermute | solution.py:26
  483.6 17.0 %copy-start.4 = (bf16[2,2,128,256]{2,3,1,0:T(8,128)(2,1)S(1)}, bf16[2,2,128,256]{2,3,1,0:T(8,128)(2,1)}, u32[]{:S(2)}) copy-start(bf16[2,2,128,256]{2,3,1,0:T(8,128)(2,1)} %copy-done.3) | copy-start | bytes 786436 | tf_op jit(solution)/shard_map/while
  504.5 1.9 collective-permute-start.2
  506.5 25.3 %collective-permute-start.3 = (bf16[128,2048]{1,0:T(8,128)(2,1)S(1)}, bf16[128,2048]{1,0:T(8,128)(2,1)}, u32[]{:S(2)}, u32[]{:S(2)}) collective-permute-start(bf16[128,2048]{1,0:T(8,128)(2,1)S(1)} %get-tuple-element.1444), channel_id=1, source_target_pairs={{32,0},{64,32},{96,64},{128,96},{160,128},{192,160},{224,192},{33,... | collective-permute-start | bytes 1572872 | tf_op jit(solution)/shard_map/while/body/eval_jaxpr/ppermute | solution.py:26
  507.8 24.0 %copy-start.4 = (bf16[2,2,128,256]{2,3,1,0:T(8,128)(2,1)S(1)}, bf16[2,2,128,256]{2,3,1,0:T(8,128)(2,1)}, u32[]{:S(2)}) copy-start(bf16[2,2,128,256]{2,3,1,0:T(8,128)(2,1)} %copy-done.3) | copy-start | bytes 786436 | tf_op jit(solution)/shard_map/while
  535.6 1.9 collective-permute-start.2
  537.6 18.3 %collective-permute-start.3 = (bf16[128,2048]{1,0:T(8,128)(2,1)S(1)}, bf16[128,2048]{1,0:T(8,128)(2,1)}, u32[]{:S(2)}, u32[]{:S(2)}) collective-permute-start(bf16[128,2048]{1,0:T(8,128)(2,1)S(1)} %get-tuple-element.1444), channel_id=1, source_target_pairs={{32,0},{64,32},{96,64},{128,96},{160,128},{192,160},{224,192},{33,... | collective-permute-start | bytes 1572872 | tf_op jit(solution)/shard_map/while/body/eval_jaxpr/ppermute | solution.py:26
  538.9 17.0 %copy-start.4 = (bf16[2,2,128,256]{2,3,1,0:T(8,128)(2,1)S(1)}, bf16[2,2,128,256]{2,3,1,0:T(8,128)(2,1)}, u32[]{:S(2)}) copy-start(bf16[2,2,128,256]{2,3,1,0:T(8,128)(2,1)} %copy-done.3) | copy-start | bytes 786436 | tf_op jit(solution)/shard_map/while
  559.8 1.9 collective-permute-start.2
  561.9 25.3 %collective-permute-start.3 = (bf16[128,2048]{1,0:T(8,128)(2,1)S(1)}, bf16[128,2048]{1,0:T(8,128)(2,1)}, u32[]{:S(2)}, u32[]{:S(2)}) collective-permute-start(bf16[128,2048]{1,0:T(8,128)(2,1)S(1)} %get-tuple-element.1444), channel_id=1, source_target_pairs={{32,0},{64,32},{96,64},{128,96},{160,128},{192,160},{224,192},{33,... | collective-permute-start | bytes 1572872 | tf_op jit(solution)/shard_map/while/body/eval_jaxpr/ppermute | solution.py:26
  563.2 24.0 %copy-start.4 = (bf16[2,2,128,256]{2,3,1,0:T(8,128)(2,1)S(1)}, bf16[2,2,128,256]{2,3,1,0:T(8,128)(2,1)}, u32[]{:S(2)}) copy-start(bf16[2,2,128,256]{2,3,1,0:T(8,128)(2,1)} %copy-done.3) | copy-start | bytes 786436 | tf_op jit(solution)/shard_map/while
  590.9 1.9 collective-permute-start.2
  593.0 17.6 %collective-permute-start.3 = (bf16[128,2048]{1,0:T(8,128)(2,1)S(1)}, bf16[128,2048]{1,0:T(8,128)(2,1)}, u32[]{:S(2)}, u32[]{:S(2)}) collective-permute-start(bf16[128,2048]{1,0:T(8,128)(2,1)S(1)} %get-tuple-element.1444), channel_id=1, source_target_pairs={{32,0},{64,32},{96,64},{128,96},{160,128},{192,160},{224,192},{33,... | collective-permute-start | bytes 1572872 | tf_op jit(solution)/shard_map/while/body/eval_jaxpr/ppermute | solution.py:26
  594.3 16.3 %copy-start.4 = (bf16[2,2,128,256]{2,3,1,0:T(8,128)(2,1)S(1)}, bf16[2,2,128,256]{2,3,1,0:T(8,128)(2,1)}, u32[]{:S(2)}) copy-start(bf16[2,2,128,256]{2,3,1,0:T(8,128)(2,1)} %copy-done.3) | copy-start | bytes 786436 | tf_op jit(solution)/shard_map/while
  614.4 1.9 collective-permute-start.2
  616.4 178.0 %collective-permute-start.3 = (bf16[128,2048]{1,0:T(8,128)(2,1)S(1)}, bf16[128,2048]{1,0:T(8,128)(2,1)}, u32[]{:S(2)}, u32[]{:S(2)}) collective-permute-start(bf16[128,2048]{1,0:T(8,128)(2,1)S(1)} %get-tuple-element.1444), channel_id=1, source_target_pairs={{32,0},{64,32},{96,64},{128,96},{160,128},{192,160},{224,192},{33,... | collective-permute-start | bytes 1572872 | tf_op jit(solution)/shard_map/while/body/eval_jaxpr/ppermute | solution.py:26
  617.7 176.7 %copy-start.4 = (bf16[2,2,128,256]{2,3,1,0:T(8,128)(2,1)S(1)}, bf16[2,2,128,256]{2,3,1,0:T(8,128)(2,1)}, u32[]{:S(2)}) copy-start(bf16[2,2,128,256]{2,3,1,0:T(8,128)(2,1)} %copy-done.3) | copy-start | bytes 786436 | tf_op jit(solution)/shard_map/while
  812.4 2.0 collective-permute-start.2
  815.7 5.3 copy-start.1
  822.6 20.6 %collective-permute-start.3 = (bf16[128,2048]{1,0:T(8,128)(2,1)S(1)}, bf16[128,2048]{1,0:T(8,128)(2,1)}, u32[]{:S(2)}, u32[]{:S(2)}) collective-permute-start(bf16[128,2048]{1,0:T(8,128)(2,1)S(1)} %get-tuple-element.1444), channel_id=1, source_target_pairs={{32,0},{64,32},{96,64},{128,96},{160,128},{192,160},{224,192},{33,... | collective-permute-start | bytes 1572872 | tf_op jit(solution)/shard_map/while/body/eval_jaxpr/ppermute | solution.py:26
  823.9 19.4 %copy-start.4 = (bf16[2,2,128,256]{2,3,1,0:T(8,128)(2,1)S(1)}, bf16[2,2,128,256]{2,3,1,0:T(8,128)(2,1)}, u32[]{:S(2)}) copy-start(bf16[2,2,128,256]{2,3,1,0:T(8,128)(2,1)} %copy-done.3) | copy-start | bytes 786436 | tf_op jit(solution)/shard_map/while
  850.0 3.9 copy-start.15
  862.1 1.9 collective-permute-start.5
  891.5 205.3 %reduce-scatter.3.cloned.1.call-start = ((), (), s32[]{:S(2)}) async-start(), calls=%async_computation.2 | async-start | bytes 6488064 | tf_op jit(solution)/shard_map/reduce_scatter | solution.py:234
  (27 other events, 63.3 us)
Sparse Core Ops, SparseCore 0:
  10.6 64.6 all-gather.4
  77.8 66.3 all-gather.6
  891.6 93.1 reduce-scatter.4
  989.2 107.5 reduce-scatter.2
where the time goes:
time: 1110 us; the launch traced here: 1100 us
  waiting for transfers between devices  720 us (65%)
  local copies, waits for them, and re-layouts  104 us (9%)
  other arithmetic  96.1 us (9%)
  starting transfers between devices  91.3 us (8%)
  matrix products  74.2 us (7%)
  between operations  13.9 us (1%)
    ppermute x16, waiting for transfers between devices, from_behind(): lax.ppermute(value, axis, [(source, source + steps) for source in range(l...  380 us
    reduce_scatter x1, waiting for transfers between devices, on_device(): lax.psum_scatter(ledger[0].astype(jnp.bfloat16), 'dp', scatter_dimension=...  110 us
    reduce_scatter x1, waiting for transfers between devices, on_device(): lax.psum_scatter(ledger[1].astype(jnp.bfloat16), 'dp', scatter_dimension=...  85.3 us
    ppermute x16, starting transfers between devices, from_behind(): lax.ppermute(value, axis, [(source, source + steps) for source in range(l...  76.2 us
    all_gather x1, waiting for transfers between devices, on_device(): lax.all_gather(w_qkv[0], 'dp', axis=0, tiled=True)  69 us
    all_gather x1, waiting for transfers between devices, on_device(): lax.all_gather(w_out[0], 'dp', axis=0, tiled=True)  65.1 us
    dynamic_update_slice x53, other arithmetic, keep_slot(): lax.dynamic_update_index_in_dim(store, jnp.where(active, value, current),...  54.4 us
    dynamic_slice x39, local copies, waits for them, and re-layouts, keep_slot(): current = lax.dynamic_index_in_dim(store, slot_index, 0, keepdims=False)  29.3 us
  transfers between devices with their start and end apart: 38, of which 29 were waited for; matrix products, arithmetic and copies ran while one was open for 8% of the time, Pallas kernels for 0%

commit v1 on v0

--- a/solution.py
+++ b/solution.py
@@ -116,7 +116,9 @@
     row_count = inputs.shape[1]
     model_width = inputs.shape[2]
     full_qkv, full_out = (
-        lax.all_gather(w_qkv[0], "dp", axis=0, tiled=True),
+        jnp.concatenate(
+            lax.all_to_all(jnp.stack([w_qkv[0]] * lax.axis_size("dp")), "dp", 0, 0), axis=0
+        ),
         lax.all_gather(w_out[0], "dp", axis=0, tiled=True),
     )
     inner_width = full_out.shape[0]

time: 1110 us -> 1150 us (1.036)
  waiting for transfers between devices: 720 us -> 735 us
  starting transfers between devices: 91.3 us -> 104 us
    all_gather x1 -> x0, waiting for transfers between devices: 69 us -> none  [on_device(): lax.all_gather(w_qkv[0], 'dp', axis=0, tiled=True)]
    all_gather x1, waiting for transfers between devices: 65.1 us -> 129 us  [on_device(): lax.all_gather(w_out[0], 'dp', axis=0, tiled=True)]
    all_to_all x0 -> x1, waiting for transfers between devices: none -> 28.5 us  [on_device(): lax.all_to_all(jnp.stack([w_qkv[0]] * lax.axis_size('dp')), 'dp', 0, 0)]
    all_to_all x0 -> x1, starting transfers between devices: none -> 12.8 us  [on_device(): lax.all_to_all(jnp.stack([w_qkv[0]] * lax.axis_size('dp')), 'dp', 0, 0)]
  transfers between devices with their start and end apart: 38 -> 38, of which waited for: 29 -> 29; matrix products, arithmetic and copies ran while one was open for 8% -> 9% of each run, Pallas kernels for 0% -> 0%
where the time goes in v1:
time: 1150 us
  waiting for transfers between devices  735 us (64%)
  local copies, waits for them, and re-layouts  114 us (10%)
  starting transfers between devices  104 us (9%)
  other arithmetic  100 us (9%)
  matrix products  74.1 us (6%)
  between operations  13.9 us (1%)
    ppermute x16, waiting for transfers between devices, from_behind(): lax.ppermute(value, axis, [(source, source + steps) for source in range(l...  370 us
    all_gather x1, waiting for transfers between devices, on_device(): lax.all_gather(w_out[0], 'dp', axis=0, tiled=True)  129 us
    reduce_scatter x1, waiting for transfers between devices, on_device(): lax.psum_scatter(ledger[0].astype(jnp.bfloat16), 'dp', scatter_dimension=...  111 us
    reduce_scatter x1, waiting for transfers between devices, on_device(): lax.psum_scatter(ledger[1].astype(jnp.bfloat16), 'dp', scatter_dimension=...  86.7 us
    ppermute x16, starting transfers between devices, from_behind(): lax.ppermute(value, axis, [(source, source + steps) for source in range(l...  76.1 us
    dynamic_update_slice x53, other arithmetic, keep_slot(): lax.dynamic_update_index_in_dim(store, jnp.where(active, value, current),...  60.5 us
    dynamic_slice x39, local copies, waits for them, and re-layouts, keep_slot(): current = lax.dynamic_index_in_dim(store, slot_index, 0, keepdims=False)  37.5 us
    all_to_all x1, waiting for transfers between devices, on_device(): lax.all_to_all(jnp.stack([w_qkv[0]] * lax.axis_size('dp')), 'dp', 0, 0)  28.5 us
  transfers between devices with their start and end apart: 38, of which 29 were waited for; matrix products, arithmetic and copies ran while one was open for 9% of the time, Pallas kernels for 0%

profile of v1, /device:TPU:1, one launch (start us, length us, event | category | flops | bytes accessed | tf_op | source)
XLA Modules:
  0.0 1146.5 jit_solution(2429352687327257727)
XLA Ops:
  7.2 4.3 stack.27
  11.5 12.8 %all-to-all-start = ((bf16[32,64,1536]{2,1,0:T(8,128)(2,1)}), bf16[32,64,1536]{2,1,0:T(8,128)(2,1)}, u32[]{:S(2)}, u32[]{:S(2)}) async-start(bf16[32,64,1536]{2,1,0:T(8,128)(2,1)} %stack.27), calls=%async_computation | async-start | bytes 12582912 | tf_op jit(solution)/shard_map/all_to_all | solution.py:120
  25.8 129.4 %all-gather.3.cloned.1.call-done = bf16[1,1024,2048]{2,1,0:T(8,128)(2,1)} async-done(((bf16[1,32,2048]{2,1,0:T(8,128)(2,1)}), bf16[1,1024,2048]{2,1,0:T(8,128)(2,1)}) %all-gather.3.cloned.1.call-update) | async-done | bytes 4194320 | tf_op jit(solution)/shard_map/all_gather | solution.py:122
  155.2 28.5 %all-to-all-done = bf16[32,64,1536]{2,1,0:T(8,128)(2,1)} async-done(((bf16[32,64,1536]{2,1,0:T(8,128)(2,1)}), bf16[32,64,1536]{2,1,0:T(8,128)(2,1)}, u32[]{:S(2)}, u32[]{:S(2)}) %all-to-all-start) | async-done | bytes 6291488 | tf_op jit(solution)/shard_map/all_to_all | solution.py:120
  188.4 273.9 %while.45 = (s32[]{:T(128)}, bf16[128,2048]{1,0:T(8,128)(2,1)S(1)}, bf16[2,128,2048]{2,1,0:T(8,128)(2,1)}, bf16[2,128,2048]{2,1,0:T(8,128)(2,1)}, bf16[2,128,102...) while((s32[]{:T(128)}, bf16[128,2048]{1,0:T(8,128)(2,1)S(1)}, ...), condition=%wide.region_7.8_spmd, body=%wide.region_0.7_spmd.sunk | while | flops 1484519552 | bytes 54158872 | solution.py:182
  191.7 6.9 conditional.20
  205.0 7.8 conditional.21
  217.4 8.0 collective-permute-done.1
  228.8 6.9 conditional.20
  242.4 7.8 conditional.21
  250.1 4.1 collective-permute-start.1
  257.6 8.0 collective-permute-done.1
  277.0 17.4 %collective-permute-start.1 = (bf16[128,2048]{1,0:T(8,128)(2,1)S(1)}, bf16[128,2048]{1,0:T(8,128)(2,1)S(1)}, u32[]{:S(2)}, u32[]{:S(2)}) collective-permute-start(bf16[128,2048]{1,0:T(8,128)(2,1)S(1)} %get-tuple-element.1417), channel_id=1, source_target_pairs={{0,32},{32,64},{64,96},{96,128},{128,160},{160,192},{192,224},{1,3... | collective-permute-start | bytes 1572872 | tf_op jit(solution)/shard_map/while/body/eval_jaxpr/ppermute | solution.py:26
  296.8 8.9 collective-permute-done.1
  317.2 4.1 collective-permute-start.1
  323.7 8.9 collective-permute-done.1
  344.1 15.2 %collective-permute-start.1 = (bf16[128,2048]{1,0:T(8,128)(2,1)S(1)}, bf16[128,2048]{1,0:T(8,128)(2,1)S(1)}, u32[]{:S(2)}, u32[]{:S(2)}) collective-permute-start(bf16[128,2048]{1,0:T(8,128)(2,1)S(1)} %get-tuple-element.1417), channel_id=1, source_target_pairs={{0,32},{32,64},{64,96},{96,128},{128,160},{160,192},{192,224},{1,3... | collective-permute-start | bytes 1572872 | tf_op jit(solution)/shard_map/while/body/eval_jaxpr/ppermute | solution.py:26
  361.7 8.9 collective-permute-done.1
  382.1 4.1 collective-permute-start.1
  388.6 8.9 collective-permute-done.1
  408.9 15.2 %collective-permute-start.1 = (bf16[128,2048]{1,0:T(8,128)(2,1)S(1)}, bf16[128,2048]{1,0:T(8,128)(2,1)S(1)}, u32[]{:S(2)}, u32[]{:S(2)}) collective-permute-start(bf16[128,2048]{1,0:T(8,128)(2,1)S(1)} %get-tuple-element.1417), channel_id=1, source_target_pairs={{0,32},{32,64},{64,96},{96,128},{128,160},{160,192},{192,224},{1,3... | collective-permute-start | bytes 1572872 | tf_op jit(solution)/shard_map/while/body/eval_jaxpr/ppermute | solution.py:26
  426.6 8.9 collective-permute-done.1
  446.9 4.1 collective-permute-start.1
  453.5 8.9 collective-permute-done.1
  477.6 6.1 broadcast_in_dim.196
  483.7 4.3 broadcast_in_dim.197
  488.8 397.8 %while.46 = (s32[]{:T(128)}, bf16[128,2048]{1,0:T(8,128)(2,1)}, f32[2048,1536]{1,0:T(8,128)}, f32[1024,2048]{1,0:T(8,128)}, s32[]{:T(128)}, /*index=5*/pred[]{:T...) while((s32[]{:T(128)}, bf16[128,2048]{1,0:T(8,128)(2,1)}, ...), condition=%wide.region_25.26_spmd, body=%wide.region_14.25_spmd.sunk | while | flops 3045198336 | bytes 89772920 | solution.py:233
  495.4 30.4 %collective-permute-done.3 = bf16[128,2048]{1,0:T(8,128)(2,1)} collective-permute-done((bf16[128,2048]{1,0:T(8,128)(2,1)S(1)}, bf16[128,2048]{1,0:T(8,128)(2,1)}, u32[]{:S(2)}, u32[]{:S(2)}) %collective-permute-start.3) | collective-permute-done | bytes 524320 | tf_op jit(solution)/shard_map/while/body/eval_jaxpr/ppermute | solution.py:26
  532.7 17.0 %collective-permute-done.3 = bf16[128,2048]{1,0:T(8,128)(2,1)} collective-permute-done((bf16[128,2048]{1,0:T(8,128)(2,1)S(1)}, bf16[128,2048]{1,0:T(8,128)(2,1)}, u32[]{:S(2)}, u32[]{:S(2)}) %collective-permute-start.3) | collective-permute-done | bytes 524320 | tf_op jit(solution)/shard_map/while/body/eval_jaxpr/ppermute | solution.py:26
  556.8 23.9 %collective-permute-done.3 = bf16[128,2048]{1,0:T(8,128)(2,1)} collective-permute-done((bf16[128,2048]{1,0:T(8,128)(2,1)S(1)}, bf16[128,2048]{1,0:T(8,128)(2,1)}, u32[]{:S(2)}, u32[]{:S(2)}) %collective-permute-start.3) | collective-permute-done | bytes 524320 | tf_op jit(solution)/shard_map/while/body/eval_jaxpr/ppermute | solution.py:26
  587.8 17.0 %collective-permute-done.3 = bf16[128,2048]{1,0:T(8,128)(2,1)} collective-permute-done((bf16[128,2048]{1,0:T(8,128)(2,1)S(1)}, bf16[128,2048]{1,0:T(8,128)(2,1)}, u32[]{:S(2)}, u32[]{:S(2)}) %collective-permute-start.3) | collective-permute-done | bytes 524320 | tf_op jit(solution)/shard_map/while/body/eval_jaxpr/ppermute | solution.py:26
  611.9 23.9 %collective-permute-done.3 = bf16[128,2048]{1,0:T(8,128)(2,1)} collective-permute-done((bf16[128,2048]{1,0:T(8,128)(2,1)S(1)}, bf16[128,2048]{1,0:T(8,128)(2,1)}, u32[]{:S(2)}, u32[]{:S(2)}) %collective-permute-start.3) | collective-permute-done | bytes 524320 | tf_op jit(solution)/shard_map/while/body/eval_jaxpr/ppermute | solution.py:26
  642.8 16.3 %collective-permute-done.3 = bf16[128,2048]{1,0:T(8,128)(2,1)} collective-permute-done((bf16[128,2048]{1,0:T(8,128)(2,1)S(1)}, bf16[128,2048]{1,0:T(8,128)(2,1)}, u32[]{:S(2)}, u32[]{:S(2)}) %collective-permute-start.3) | collective-permute-done | bytes 524320 | tf_op jit(solution)/shard_map/while/body/eval_jaxpr/ppermute | solution.py:26
  666.2 172.5 %collective-permute-done.3 = bf16[128,2048]{1,0:T(8,128)(2,1)} collective-permute-done((bf16[128,2048]{1,0:T(8,128)(2,1)S(1)}, bf16[128,2048]{1,0:T(8,128)(2,1)}, u32[]{:S(2)}, u32[]{:S(2)}) %collective-permute-start.3) | collective-permute-done | bytes 524320 | tf_op jit(solution)/shard_map/while/body/eval_jaxpr/ppermute | solution.py:26
  840.0 15.0 %conditional.22 = (bf16[128,1024]{0,1:T(8,128)(2,1)}, bf16[2,128,256]{1,2,0:T(8,128)(2,1)S(1)}, bf16[2,128,256]{1,2,0:T(8,128)(2,1)}) conditional(s32[]{:T(128)} %convert_element_type.320, () %tuple.239, (bf16[128,2048]{1,0:T(8,128)(2,1)S(1)}, bf16[1024,2048]{1,0:T(8,128)(2,1)}, bf16[2,2,128,256]{2,3,1,0:T(8,128)(2,1)}, s32[]{:T(128)}, ...), branch_computations={%region_15.15_spmd, %region_16.18_spmd} | conditional | flops 887359488 | bytes 25409794 | solution.py:205
  858.0 8.2 conditional.23
  859.3 5.2 fusion.41
  867.4 19.1 %conditional.24 = ((f32[2048,1536]{1,0:T(8,128)}, f32[1024,2048]{1,0:T(8,128)})) conditional(s32[]{:T(128)} %convert_element_type.320, (f32[2048,1536]{1,0:T(8,128)}, f32[1024,2048]{1,0:T(8,128)}) %tuple.242, (bf16[2,128,2048]{2,1,0:T(8,128)(2,1)}, s32[]{:T(128)}, bf16[128,1536]{1,0:T(8,128)(2,1)S(1)}, f32[2048,1536]{1,0:T(8,128)}, ...), branch_computations={%region_23.23_spmd, %region_24.24_spmd} | conditional | flops 1347420160 | bytes 43648024 | solution.py:226
  867.5 11.1 convolution_add_fusion.1
  878.6 8.0 convolution_add_fusion.2
  888.0 14.8 %conditional.12 = (bf16[128,1024]{0,1:T(8,128)(2,1)}, bf16[2,128,256]{1,2,0:T(8,128)(2,1)S(1)}, bf16[2,128,256]{1,2,0:T(8,128)(2,1)S(1)}) conditional(s32[]{:T(128)} %convert_element_type.228, () %tuple.147, (bf16[128,2048]{1,0:T(8,128)(2,1)S(1)}, bf16[1024,2048]{1,0:T(8,128)(2,1)}, bf16[2,2,128,256]{2,3,1,0:T(8,128)(2,1)}, s32[]{:T(128)}, ...), branch_computations={%region_26.27_spmd, %region_27.30_spmd} | conditional | flops 887359488 | bytes 25409810 | solution.py:205
  906.2 19.1 %conditional.14 = ((f32[2048,1536]{1,0:T(8,128)}, f32[1024,2048]{1,0:T(8,128)})) conditional(s32[]{:T(128)} %convert_element_type.228, (f32[2048,1536]{1,0:T(8,128)}, f32[1024,2048]{1,0:T(8,128)}) %tuple.145, (bf16[2,128,2048]{2,1,0:T(8,128)(2,1)}, s32[]{:T(128)}, bf16[128,1536]{1,0:T(8,128)(2,1)S(1)}, f32[2048,1536]{1,0:T(8,128)}, ...), branch_computations={%region_32.33_spmd, %region_33.34_spmd} | conditional | flops 1347420160 | bytes 43648024 | solution.py:226
  906.2 11.1 convolution_add_fusion.3
  917.3 8.0 convolution_add_fusion.4
  925.3 6.1 convert_element_type.231
  931.4 8.0 convert_element_type.230
  939.4 86.7 %reduce-scatter.5.cloned.1.call-done = bf16[32,2048]{1,0:T(8,128)(2,1)} async-done(((bf16[1024,2048]{1,0:T(8,128)(2,1)}), bf16[32,2048]{1,0:T(8,128)(2,1)}) %reduce-scatter.5.cloned.1.call-update) | async-done | bytes 131088 | tf_op jit(solution)/shard_map/reduce_scatter | solution.py:239
  1027.7 110.6 %reduce-scatter.3.cloned.1.call-done = bf16[64,1536]{1,0:T(8,128)(2,1)} async-done(((bf16[2048,1536]{1,0:T(8,128)(2,1)}), bf16[64,1536]{1,0:T(8,128)(2,1)}) %reduce-scatter.3.cloned.1.call-update) | async-done | bytes 196624 | tf_op jit(solution)/shard_map/reduce_scatter | solution.py:236
  (418 shorter events, 280.9 us)
Async XLA Ops:
  11.5 13.6 %copy-start.15 = (s32[2,16]{1,0:T(2,128)S(1)}, s32[2,16]{1,0:T(2,128)}, u32[]{:S(2)}) copy-start(s32[2,16]{1,0:T(2,128)} %param.31) | copy-start | bytes 388
  11.5 172.2 %all-to-all-start = ((bf16[32,64,1536]{2,1,0:T(8,128)(2,1)}), bf16[32,64,1536]{2,1,0:T(8,128)(2,1)}, u32[]{:S(2)}, u32[]{:S(2)}) async-start(bf16[32,64,1536]{2,1,0:T(8,128)(2,1)} %stack.27), calls=%async_computation | async-start | bytes 12582912 | tf_op jit(solution)/shard_map/all_to_all | solution.py:120
  24.3 130.9 %all-gather.3.cloned.1.call-start = ((), (), s32[]{:S(2)}) async-start(), calls=%async_computation.5 | async-start | bytes 4325376 | tf_op jit(solution)/shard_map/all_gather | solution.py:122
  25.0 1001.1 %reduce-scatter.5.cloned.1.call-start = ((), (), s32[]{:S(2)}) async-start(), calls=%async_computation.4 | async-start | bytes 4325376 | tf_op jit(solution)/shard_map/reduce_scatter | solution.py:239
  198.6 6.4 collective-permute-start
  208.8 2.3 copy-start
  212.8 12.7 %collective-permute-start.1 = (bf16[128,2048]{1,0:T(8,128)(2,1)S(1)}, bf16[128,2048]{1,0:T(8,128)(2,1)S(1)}, u32[]{:S(2)}, u32[]{:S(2)}) collective-permute-start(bf16[128,2048]{1,0:T(8,128)(2,1)S(1)} %get-tuple-element.1417), channel_id=1, source_target_pairs={{0,32},{32,64},{64,96},{96,128},{128,160},{160,192},{192,224},{1,3... | collective-permute-start | bytes 1572872 | tf_op jit(solution)/shard_map/while/body/eval_jaxpr/ppermute | solution.py:26
  235.7 6.7 collective-permute-start
  246.2 2.3 copy-start
  250.1 15.4 %collective-permute-start.1 = (bf16[128,2048]{1,0:T(8,128)(2,1)S(1)}, bf16[128,2048]{1,0:T(8,128)(2,1)S(1)}, u32[]{:S(2)}, u32[]{:S(2)}) collective-permute-start(bf16[128,2048]{1,0:T(8,128)(2,1)S(1)} %get-tuple-element.1417), channel_id=1, source_target_pairs={{0,32},{32,64},{64,96},{96,128},{128,160},{160,192},{192,224},{1,3... | collective-permute-start | bytes 1572872 | tf_op jit(solution)/shard_map/while/body/eval_jaxpr/ppermute | solution.py:26
  270.4 5.8 collective-permute-start
  277.0 28.7 %collective-permute-start.1 = (bf16[128,2048]{1,0:T(8,128)(2,1)S(1)}, bf16[128,2048]{1,0:T(8,128)(2,1)S(1)}, u32[]{:S(2)}, u32[]{:S(2)}) collective-permute-start(bf16[128,2048]{1,0:T(8,128)(2,1)S(1)} %get-tuple-element.1417), channel_id=1, source_target_pairs={{0,32},{32,64},{64,96},{96,128},{128,160},{160,192},{192,224},{1,3... | collective-permute-start | bytes 1572872 | tf_op jit(solution)/shard_map/while/body/eval_jaxpr/ppermute | solution.py:26
  310.6 5.8 collective-permute-start
  317.2 15.4 %collective-permute-start.1 = (bf16[128,2048]{1,0:T(8,128)(2,1)S(1)}, bf16[128,2048]{1,0:T(8,128)(2,1)S(1)}, u32[]{:S(2)}, u32[]{:S(2)}) collective-permute-start(bf16[128,2048]{1,0:T(8,128)(2,1)S(1)} %get-tuple-element.1417), channel_id=1, source_target_pairs={{0,32},{32,64},{64,96},{96,128},{128,160},{160,192},{192,224},{1,3... | collective-permute-start | bytes 1572872 | tf_op jit(solution)/shard_map/while/body/eval_jaxpr/ppermute | solution.py:26
  337.5 5.8 collective-permute-start
  344.1 26.5 %collective-permute-start.1 = (bf16[128,2048]{1,0:T(8,128)(2,1)S(1)}, bf16[128,2048]{1,0:T(8,128)(2,1)S(1)}, u32[]{:S(2)}, u32[]{:S(2)}) collective-permute-start(bf16[128,2048]{1,0:T(8,128)(2,1)S(1)} %get-tuple-element.1417), channel_id=1, source_target_pairs={{0,32},{32,64},{64,96},{96,128},{128,160},{160,192},{192,224},{1,3... | collective-permute-start | bytes 1572872 | tf_op jit(solution)/shard_map/while/body/eval_jaxpr/ppermute | solution.py:26
  375.5 5.8 collective-permute-start
  382.1 15.4 %collective-permute-start.1 = (bf16[128,2048]{1,0:T(8,128)(2,1)S(1)}, bf16[128,2048]{1,0:T(8,128)(2,1)S(1)}, u32[]{:S(2)}, u32[]{:S(2)}) collective-permute-start(bf16[128,2048]{1,0:T(8,128)(2,1)S(1)} %get-tuple-element.1417), channel_id=1, source_target_pairs={{0,32},{32,64},{64,96},{96,128},{128,160},{160,192},{192,224},{1,3... | collective-permute-start | bytes 1572872 | tf_op jit(solution)/shard_map/while/body/eval_jaxpr/ppermute | solution.py:26
  402.3 5.8 collective-permute-start
  408.9 26.5 %collective-permute-start.1 = (bf16[128,2048]{1,0:T(8,128)(2,1)S(1)}, bf16[128,2048]{1,0:T(8,128)(2,1)S(1)}, u32[]{:S(2)}, u32[]{:S(2)}) collective-permute-start(bf16[128,2048]{1,0:T(8,128)(2,1)S(1)} %get-tuple-element.1417), channel_id=1, source_target_pairs={{0,32},{32,64},{64,96},{96,128},{128,160},{160,192},{192,224},{1,3... | collective-permute-start | bytes 1572872 | tf_op jit(solution)/shard_map/while/body/eval_jaxpr/ppermute | solution.py:26
  440.3 5.8 collective-permute-start
  446.9 15.4 %collective-permute-start.1 = (bf16[128,2048]{1,0:T(8,128)(2,1)S(1)}, bf16[128,2048]{1,0:T(8,128)(2,1)S(1)}, u32[]{:S(2)}, u32[]{:S(2)}) collective-permute-start(bf16[128,2048]{1,0:T(8,128)(2,1)S(1)} %get-tuple-element.1417), channel_id=1, source_target_pairs={{0,32},{32,64},{64,96},{96,128},{128,160},{160,192},{192,224},{1,3... | collective-permute-start | bytes 1572872 | tf_op jit(solution)/shard_map/while/body/eval_jaxpr/ppermute | solution.py:26
  467.2 8.7 collective-permute-start.4
  492.6 1.4 collective-permute-start.2
  494.1 31.7 %collective-permute-start.3 = (bf16[128,2048]{1,0:T(8,128)(2,1)S(1)}, bf16[128,2048]{1,0:T(8,128)(2,1)}, u32[]{:S(2)}, u32[]{:S(2)}) collective-permute-start(bf16[128,2048]{1,0:T(8,128)(2,1)S(1)} %get-tuple-element.1444), channel_id=1, source_target_pairs={{32,0},{64,32},{96,64},{128,96},{160,128},{192,160},{224,192},{33,... | collective-permute-start | bytes 1572872 | tf_op jit(solution)/shard_map/while/body/eval_jaxpr/ppermute | solution.py:26
  529.5 1.8 collective-permute-start.2
  531.4 18.3 %collective-permute-start.3 = (bf16[128,2048]{1,0:T(8,128)(2,1)S(1)}, bf16[128,2048]{1,0:T(8,128)(2,1)}, u32[]{:S(2)}, u32[]{:S(2)}) collective-permute-start(bf16[128,2048]{1,0:T(8,128)(2,1)S(1)} %get-tuple-element.1444), channel_id=1, source_target_pairs={{32,0},{64,32},{96,64},{128,96},{160,128},{192,160},{224,192},{33,... | collective-permute-start | bytes 1572872 | tf_op jit(solution)/shard_map/while/body/eval_jaxpr/ppermute | solution.py:26
  553.4 1.9 collective-permute-start.2
  555.5 25.2 %collective-permute-start.3 = (bf16[128,2048]{1,0:T(8,128)(2,1)S(1)}, bf16[128,2048]{1,0:T(8,128)(2,1)}, u32[]{:S(2)}, u32[]{:S(2)}) collective-permute-start(bf16[128,2048]{1,0:T(8,128)(2,1)S(1)} %get-tuple-element.1444), channel_id=1, source_target_pairs={{32,0},{64,32},{96,64},{128,96},{160,128},{192,160},{224,192},{33,... | collective-permute-start | bytes 1572872 | tf_op jit(solution)/shard_map/while/body/eval_jaxpr/ppermute | solution.py:26
  584.4 1.9 collective-permute-start.2
  586.4 18.3 %collective-permute-start.3 = (bf16[128,2048]{1,0:T(8,128)(2,1)S(1)}, bf16[128,2048]{1,0:T(8,128)(2,1)}, u32[]{:S(2)}, u32[]{:S(2)}) collective-permute-start(bf16[128,2048]{1,0:T(8,128)(2,1)S(1)} %get-tuple-element.1444), channel_id=1, source_target_pairs={{32,0},{64,32},{96,64},{128,96},{160,128},{192,160},{224,192},{33,... | collective-permute-start | bytes 1572872 | tf_op jit(solution)/shard_map/while/body/eval_jaxpr/ppermute | solution.py:26
  608.5 1.9 collective-permute-start.2
  610.5 25.2 %collective-permute-start.3 = (bf16[128,2048]{1,0:T(8,128)(2,1)S(1)}, bf16[128,2048]{1,0:T(8,128)(2,1)}, u32[]{:S(2)}, u32[]{:S(2)}) collective-permute-start(bf16[128,2048]{1,0:T(8,128)(2,1)S(1)} %get-tuple-element.1444), channel_id=1, source_target_pairs={{32,0},{64,32},{96,64},{128,96},{160,128},{192,160},{224,192},{33,... | collective-permute-start | bytes 1572872 | tf_op jit(solution)/shard_map/while/body/eval_jaxpr/ppermute | solution.py:26
  639.5 1.9 collective-permute-start.2
  641.5 17.6 %collective-permute-start.3 = (bf16[128,2048]{1,0:T(8,128)(2,1)S(1)}, bf16[128,2048]{1,0:T(8,128)(2,1)}, u32[]{:S(2)}, u32[]{:S(2)}) collective-permute-start(bf16[128,2048]{1,0:T(8,128)(2,1)S(1)} %get-tuple-element.1444), channel_id=1, source_target_pairs={{32,0},{64,32},{96,64},{128,96},{160,128},{192,160},{224,192},{33,... | collective-permute-start | bytes 1572872 | tf_op jit(solution)/shard_map/while/body/eval_jaxpr/ppermute | solution.py:26
  662.8 1.9 collective-permute-start.2
  664.8 173.9 %collective-permute-start.3 = (bf16[128,2048]{1,0:T(8,128)(2,1)S(1)}, bf16[128,2048]{1,0:T(8,128)(2,1)}, u32[]{:S(2)}, u32[]{:S(2)}) collective-permute-start(bf16[128,2048]{1,0:T(8,128)(2,1)S(1)} %get-tuple-element.1444), channel_id=1, source_target_pairs={{32,0},{64,32},{96,64},{128,96},{160,128},{192,160},{224,192},{33,... | collective-permute-start | bytes 1572872 | tf_op jit(solution)/shard_map/while/body/eval_jaxpr/ppermute | solution.py:26
  841.0 3.6 copy-start.3
  841.0 3.6 copy-start.5
  849.0 2.4 copy-start.12
  856.0 1.9 collective-permute-start.2
  859.3 5.2 copy-start.1
  866.1 20.6 %collective-permute-start.3 = (bf16[128,2048]{1,0:T(8,128)(2,1)S(1)}, bf16[128,2048]{1,0:T(8,128)(2,1)}, u32[]{:S(2)}, u32[]{:S(2)}) collective-permute-start(bf16[128,2048]{1,0:T(8,128)(2,1)S(1)} %get-tuple-element.1444), channel_id=1, source_target_pairs={{32,0},{64,32},{96,64},{128,96},{160,128},{192,160},{224,192},{33,... | collective-permute-start | bytes 1572872 | tf_op jit(solution)/shard_map/while/body/eval_jaxpr/ppermute | solution.py:26
  889.2 3.8 copy-start.7
  889.2 3.8 copy-start.9
  897.4 2.4 copy-start.14
  902.9 1.9 collective-permute-start.5
  931.4 206.9 %reduce-scatter.3.cloned.1.call-start = ((), (), s32[]{:S(2)}) async-start(), calls=%async_computation.3 | async-start | bytes 6488064 | tf_op jit(solution)/shard_map/reduce_scatter | solution.py:236
  (7 other events, 11.2 us)
Sparse Core Ops, SparseCore 0:
  27.6 127.4 all-gather.2
  931.5 94.5 reduce-scatter.4
  1030.6 107.5 reduce-scatter.2
